TPU v7x, 32 devices: a whole 2x2x4 slice. The times are simulated.
32 devices in a mesh: size: 4 (over z), gz: 8 (over y, x, core).
Axes of the slice: x: 2, y: 2, z: 4, core: 2. Of those that a mesh axis runs over, the one named last changes fastest.
Arguments:
- tissue: int32 [256, 64, 128], P('gz'), may hold values from 0 to 2
- vessel_pressure: float32 [256, 64, 128], P('gz', 'size'), may hold values from -12 to 12
- cond_table: float32 [3], replicated, may hold values from 0.4 to 1.2
- leak_table: float32 [3], replicated, may hold values from 0.2 to 2
- bind_table: float32 [4, 3], P('size'), may hold values from 0.05 to 1
- hindrance: float32 [4], P('size'), may hold values from 0.2 to 1
- diffusivity: float32 [4], P('size'), may hold values from 0.1 to 0.6
- free_conc: float32 [4, 256, 64, 128], P('size', 'gz'), may hold values from 0 to 2
- bound_conc: float32 [4, 256, 64, 128], P('size', 'gz'), may hold values from 0 to 1
Outputs:
- pressure: float32 [256, 64, 128], P('gz', 'size')
- free_out: float32 [4, 256, 64, 128], P('size', 'gz')
- bound_out: float32 [4, 256, 64, 128], P('size', 'gz')
Inputs may be any that keep to these rules, and one draw needn't show every extreme that they name: 0 marks a vessel cell, 1 necrotic tissue, 2 viable tissue.
All inputs are finite; a program needn't handle non-finite values.
Results may differ from a plain program's by a relative error of at most 0.0001.
Values sent between devices are 32-bit elements; how exact they have to be, the bound alone decides.
No kernel may reach another device: no remote copies, remote signals or barrier semaphores. Data moves between devices by JAX's collectives and lax.ppermute only.
A program may use at most 128 MiB of HBM per device.

v0:
```python
import jax
import jax.numpy as jnp
from jax import lax
from jax.sharding import PartitionSpec as P

ITERS = 2
TSTEPS = 2
time_step = 0.1


def extended(cells, sides, width):
    for axis, dim in sides:
        count = lax.axis_size(axis)
        ends = count - 1
        head = lax.slice_in_dim(cells, 0, width, axis=dim)
        tail = lax.slice_in_dim(cells, cells.shape[dim] - width, cells.shape[dim], axis=dim)
        cells = jnp.concatenate(
            [
                lax.ppermute(tail, axis, [(i, (i + 1) % count) for i in range(ends)]),
                cells,
                lax.ppermute(head, axis, [((i + 1) % count, i) for i in range(ends)]),
            ],
            axis=dim,
        )
    return cells


def lookup(table, labels):
    return jnp.where(labels == 0, table[0], jnp.where(labels == 1, table[1], table[2]))


def neighbours(padded):
    total = padded[2:, 1:-1, 1:-1] + padded[:-2, 1:-1, 1:-1]
    total = total + padded[1:-1, 2:, 1:-1] + padded[1:-1, :-2, 1:-1]
    total = total + padded[1:-1, 1:-1, 2:] + padded[1:-1, 1:-1, :-2]
    return total


def apply_operator(vector, conduct, leak):
    scaled = conduct * vector
    rimmed = extended(scaled, (("size", 1), ("gz", 0)), 1)
    padded = jnp.pad(rimmed, ((0, 0), (0, 0), (1, 1)))
    return conduct * (6.0 * scaled - neighbours(padded)) + leak * vector


def paired_products(residual, precond, image):
    return lax.psum((jnp.sum(residual * precond), jnp.sum(precond * image)), ("size", "gz"))


def along_line(array, along_dim):
    return array[tuple((slice(None) if k == along_dim else slice(1, -1) for k in range(3)))]


def lower_part(array, along_dim):
    return array[tuple((slice(0, -1) if k == along_dim else slice(None) for k in range(3)))]


def upper_part(array, along_dim):
    return array[tuple((slice(1, None) if k == along_dim else slice(None) for k in range(3)))]


def transport_step(conc_pad, fields_pad, hinder, diffuse):
    divergence = None
    for along_dim in range(3):
        conc_line = along_line(conc_pad, along_dim)
        press_line = along_line(fields_pad[0], along_dim)
        cond_line = along_line(fields_pad[1], along_dim)
        conc_low = lower_part(conc_line, along_dim)
        conc_high = upper_part(conc_line, along_dim)
        velocity = (
            hinder
            * lower_part(cond_line, along_dim)
            * upper_part(cond_line, along_dim)
            * (lower_part(press_line, along_dim) - upper_part(press_line, along_dim))
        )
        flux = (
            jnp.maximum(velocity, 0.0) * conc_low
            + jnp.minimum(velocity, 0.0) * conc_high
            + diffuse * (conc_low - conc_high)
        )
        term = upper_part(flux, along_dim) - lower_part(flux, along_dim)
        divergence = term if divergence is None else divergence + term
    conc = conc_pad[1:-1, 1:-1, 1:-1]
    rate = fields_pad[2][1:-1, 1:-1, 1:-1]
    bind = rate * conc
    return (conc - time_step * (divergence + bind), bind)


def pad_plane(array):
    return jnp.pad(array, ((0, 0), (1, 1), (1, 1)))


def local(
    tissue,
    vessel_pressure,
    cond_table,
    leak_table,
    bind_table,
    hindrance,
    diffusivity,
    free_conc,
    bound_conc,
):
    block_x = vessel_pressure.shape[1]
    slab_z = vessel_pressure.shape[0]
    local_tissue = lax.dynamic_slice_in_dim(tissue, lax.axis_index("size") * block_x, block_x, 1)
    conduct = lookup(cond_table, local_tissue)
    leak = lookup(leak_table, local_tissue)
    diag = 6.0 * conduct * conduct + leak
    source = leak * vessel_pressure
    solution = jnp.zeros_like(source)
    residual = source
    precond = residual / diag
    image = apply_operator(precond, conduct, leak)
    rho_now, product = paired_products(residual, precond, image)
    alpha = rho_now / product
    direction = precond
    along_image = image
    for iteration in range(ITERS):
        solution = solution + alpha * direction
        residual = residual - alpha * along_image
        if iteration + 1 < ITERS:
            precond = residual / diag
            image = apply_operator(precond, conduct, leak)
            rho_next, product = paired_products(residual, precond, image)
            ratio = rho_next / rho_now
            alpha = rho_next / (product - ratio * rho_next / alpha)
            direction = precond + ratio * direction
            along_image = image + ratio * along_image
            rho_now = rho_next
    conduct_slab = lookup(cond_table, tissue)
    rate_slab = lookup(bind_table[0], tissue)
    slab_pressure = lax.all_gather(solution, "size", axis=1, tiled=True)
    stacked = jnp.stack([slab_pressure, conduct_slab, rate_slab])
    rimmed = extended(stacked, (("gz", 1),), TSTEPS)
    fields_pad = jnp.pad(rimmed, ((0, 0), (0, 0), (1, 1), (1, 1)))
    hinder = hindrance[0]
    diffuse = diffusivity[0]
    conc = free_conc[0]
    bound = bound_conc[0]
    fields_one = fields_pad[:, TSTEPS - 1 : TSTEPS + 1 + slab_z]
    for sweep in range(TSTEPS):
        conc_pad = pad_plane(extended(conc, (("gz", 0),), 1))
        conc, bind = transport_step(conc_pad, fields_one, hinder, diffuse)
        bound = bound + time_step * bind
    return (solution, conc[None], bound[None])


def solution(mesh):
    return jax.shard_map(
        local,
        mesh=mesh,
        in_specs=(
            P("gz", None, None),
            P("gz", "size", None),
            P(),
            P(),
            P("size", None),
            P("size"),
            P("size"),
            P("size", "gz", None, None),
            P("size", "gz", None, None),
        ),
        out_specs=(P("gz", "size", None), P("size", "gz", None, None), P("size", "gz", None, None)),
        check_vma=False,
    )
```

profile of v0, /device:TPU:4, one launch (start us, length us, event | category | flops | bytes accessed | tf_op | source)
XLA Modules:
  0.0 228.2 jit_solution(11120340233154857061)
XLA Ops:
  7.2 0.0 copy-start.1
  7.2 0.0 all-gather.2.cloned.1.call-start
  7.2 1.3 fusion.53
  8.6 1.4 fusion.52
  10.0 4.9 %fusion.39 = (f32[32,16,128]{2,1,0:T(8,128)S(1)}, pred[32,16,128]{2,1,0:T(8,128)(4,1)S(1)}, pred[32,16,128]{2,1,0:T(8,128)(4,1)S(1)}) fusion(f32[]{:T(128)} %bitcast.5, f32[]{:T(128)} %bitcast.4, f32[]{:T(128)} %bitcast.3, f32[32,16,128]{2,1,0:T(8,128)} %param.10, f32[]{:T(128)} %bitcast.2, f32[]{:T(128)} %bitcast.1, f32[]{:T(128)} %bitcast, ...), kind=kLoop, calls=%fused_computation.127 | loop fusion | flops 786432 | bytes 917532 | tf_op jit(solution)/shard_map/mul | solution.py:40
  15.0 1.3 collective-permute-start.1
  16.3 4.5 %collective-permute-start = (f32[32,1,128]{2,1,0:T(1,128)S(1)}, f32[32,1,128]{2,1,0:T(1,128)S(1)}, u32[]{:S(2)}, u32[]{:S(2)}) collective-permute-start(f32[32,1,128]{2,1,0:T(1,128)S(1)} %get-tuple-element.41), channel_id=1, source_target_pairs={{0,8},{8,16},{16,24},{1,9},{9,17},{17,25},{2,10},{10,18},{18,26},{... | collective-permute-start | bytes 49160 | tf_op jit(solution)/shard_map/ppermute | solution.py:19
  20.8 1.4 collective-permute-done
  22.2 1.9 collective-permute-start.2
  24.2 2.4 %collective-permute-start.3 = (f32[1,18,128]{2,1,0:T(8,128)S(1)}, f32[1,18,128]{2,1,0:T(8,128)S(1)}, u32[]{:S(2)}, u32[]{:S(2)}) collective-permute-start(f32[1,18,128]{2,1,0:T(8,128)S(1)} %get-tuple-element.37), channel_id=1, source_target_pairs={{0,1},{1,2},{2,3},{3,4},{4,5},{5,6},{6,7},{8,9},{9,10},{10,11},{11... | collective-permute-start | bytes 27656 | tf_op jit(solution)/shard_map/ppermute | solution.py:19
  26.6 3.5 %collective-permute-done.3 = f32[1,18,128]{2,1,0:T(8,128)S(1)} collective-permute-done((f32[1,18,128]{2,1,0:T(8,128)S(1)}, f32[1,18,128]{2,1,0:T(8,128)S(1)}, u32[]{:S(2)}, u32[]{:S(2)}) %collective-permute-start.3) | collective-permute-done | bytes 9248 | tf_op jit(solution)/shard_map/ppermute | solution.py:19
  30.1 0.4 select_maximum_fusion.12
  30.5 4.7 %multiply_reduce_fusion.1 = (f32[]{:T(128)}, f32[]{:T(128)}, f32[32,16,128]{2,1,0:T(8,128)S(1)}) fusion(pred[32,16,128]{2,1,0:T(8,128)(4,1)S(1)} %get-tuple-element.23, pred[32,16,128]{2,1,0:T(8,128)(4,1)S(1)} %get-tuple-element.22, f32[]{:T(128)} %bitcast.5, f32[]{:T(128)} %bitcast.4, f32[]{:T(128)} %bitcast.3, f32[32,16,128]{2,1,0:T(8,128)S(1)} %copy-done.1, ...), kind=kLoop, calls=%fused_computation.123 | loop fusion | flops 2031614 | bytes 1493024 | tf_op jit(solution)/shard_map/reduce_sum | solution.py:47
  35.3 41.6 %all-reduce.6 = (f32[]{:T(128)}, f32[]{:T(128)}) all-reduce(f32[]{:T(128)} %get-tuple-element.4, f32[]{:T(128)} %get-tuple-element.3), channel_id=1, replica_groups=mesh['size'=4,'gz'=8] {'size','gz'}, use_global_device_ids=true, to_apply=%region_1.2 | all-reduce | flops 2 | bytes 16 | tf_op jit(solution)/shard_map/psum | solution.py:47
  78.1 4.5 %fusion.38 = (f32[32,16,128]{2,1,0:T(8,128)S(1)}, f32[]{:T(128)}) fusion(pred[32,16,128]{2,1,0:T(8,128)(4,1)S(1)} %get-tuple-element.23, pred[32,16,128]{2,1,0:T(8,128)(4,1)S(1)} %get-tuple-element.22, f32[]{:T(128)} %bitcast.5, f32[]{:T(128)} %bitcast.4, f32[]{:T(128)} %bitcast.3, f32[32,16,128]{2,1,0:T(8,128)S(1)} %get-tuple-element.20, f32[]{:T(128)S(6)} %div.19, ...), kind=kLoop, calls=%fused_computation.126 | loop fusion | flops 917503 | bytes 917536 | tf_op jit(solution)/shard_map/mul | solution.py:40
  82.7 0.0 copy-start
  82.7 1.4 collective-permute-start.5
  84.1 0.0 copy-start.9
  84.1 0.0 copy-start.3
  84.2 4.7 %collective-permute-start.4 = (f32[32,1,128]{2,1,0:T(1,128)S(1)}, f32[32,1,128]{2,1,0:T(1,128)S(1)}, u32[]{:S(2)}, u32[]{:S(2)}) collective-permute-start(f32[32,1,128]{2,1,0:T(1,128)S(1)} %get-tuple-element.39), channel_id=1, source_target_pairs={{0,8},{8,16},{16,24},{1,9},{9,17},{17,25},{2,10},{10,18},{18,26},{... | collective-permute-start | bytes 49160 | tf_op jit(solution)/shard_map/ppermute | solution.py:19
  88.8 0.0 collective-permute-done.5
  88.8 1.4 collective-permute-done.4
  90.3 1.9 collective-permute-start.6
  92.2 2.4 %collective-permute-start.7 = (f32[1,18,128]{2,1,0:T(8,128)S(1)}, f32[1,18,128]{2,1,0:T(8,128)S(1)}, u32[]{:S(2)}, u32[]{:S(2)}) collective-permute-start(f32[1,18,128]{2,1,0:T(8,128)S(1)} %get-tuple-element.35), channel_id=1, source_target_pairs={{0,1},{1,2},{2,3},{3,4},{4,5},{5,6},{6,7},{8,9},{9,10},{10,11},{11... | collective-permute-start | bytes 27656 | tf_op jit(solution)/shard_map/ppermute | solution.py:19
  94.6 0.0 collective-permute-done.6
  94.6 3.5 %collective-permute-done.7 = f32[1,18,128]{2,1,0:T(8,128)S(1)} collective-permute-done((f32[1,18,128]{2,1,0:T(8,128)S(1)}, f32[1,18,128]{2,1,0:T(8,128)S(1)}, u32[]{:S(2)}, u32[]{:S(2)}) %collective-permute-start.7) | collective-permute-done | bytes 9248 | tf_op jit(solution)/shard_map/ppermute | solution.py:19
  98.1 0.4 select_maximum_fusion.8
  98.5 4.8 %fusion.28 = f32[]{:T(128)} fusion(f32[34,18,130]{2,1,0:T(8,128)S(1)} %select_maximum_fusion.8, f32[32,16,128]{2,1,0:T(8,128)S(1)} %get-tuple-element.33, f32[32,1,128]{2,1,0:T(1,128)S(1)} %collective-permute-done.4, f32[32,1,128]{2,1,0:T(1,128)S(1)} %collective-permute-done.5, f32[1,18,128]{2,1,0:T(8,128)S(1)} %collective-permute-done.7, ...), kind=kLoop, calls=%fused_computation.91 | loop fusion | flops 2031615 | bytes 1493024 | tf_op jit(solution)/shard_map/reduce_sum | solution.py:47
  103.3 41.4 %all-reduce.5 = (f32[]{:T(128)}, f32[]{:T(128)}) all-reduce(f32[]{:T(128)} %get-tuple-element.34, f32[]{:T(128)} %fusion.28), channel_id=1, replica_groups=mesh['size'=4,'gz'=8] {'size','gz'}, use_global_device_ids=true, to_apply=%region_5.6 | all-reduce | flops 2 | bytes 16 | tf_op jit(solution)/shard_map/psum | solution.py:47
  149.1 4.6 %multiply_add_fusion.6 = f32[32,16,128]{2,1,0:T(8,128)} fusion(f32[]{:T(128)S(6)} %div.21, f32[]{:T(128)S(6)} %div.23, f32[]{:T(128)S(6)} %div.19, pred[32,16,128]{2,1,0:T(8,128)(4,1)S(1)} %get-tuple-element.23, pred[32,16,128]{2,1,0:T(8,128)(4,1)S(1)} %get-tuple-element.22, f32[]{:T(128)} %bitcast.5, f32[]{:T(128)} %bitcast.4, f32[]{:T(128)} %bitcast.3, ...), kind=kLoop, calls=%fused_computation.120 | loop fusion | flops 1114112 | bytes 917540 | tf_op jit(solution)/shard_map/add | solution.py:120
  153.7 0.0 all-gather.2.cloned.1.call-update
  153.7 2.0 collective-permute-start.11
  155.7 2.3 %collective-permute-start.10 = (f32[1,64,128]{2,1,0:T(8,128)S(1)}, f32[1,64,128]{2,1,0:T(8,128)S(1)}, u32[]{:S(2)}, u32[]{:S(2)}) collective-permute-start(f32[1,64,128]{2,1,0:T(8,128)S(1)} %get-tuple-element.31), channel_id=1, source_target_pairs={{0,1},{1,2},{2,3},{3,4},{4,5},{5,6},{6,7},{8,9},{9,10},{10,11},{11... | collective-permute-start | bytes 98312 | tf_op jit(solution)/shard_map/ppermute | solution.py:19
  159.4 0.6 fusion.51
  160.0 2.2 select_bitcast_fusion.1
  162.2 2.0 select_bitcast_fusion
  164.3 17.5 %all-gather.2.cloned.1.call-done = f32[32,64,128]{2,1,0:T(8,128)} async-done(((f32[32,16,128]{2,1,0:T(8,128)}), f32[32,64,128]{2,1,0:T(8,128)}) %all-gather.2.cloned.1.call-update) | async-done | bytes 1048592 | tf_op jit(solution)/shard_map/all_gather | solution.py:133
  181.7 0.9 pad_maximum_fusion.22
  182.7 2.4 %collective-permute-start.9 = (f32[3,2,64,128]{3,2,1,0:T(8,128)S(1)}, f32[3,2,64,128]{3,2,1,0:T(8,128)S(1)}, u32[]{:S(2)}, u32[]{:S(2)}) collective-permute-start(f32[3,2,64,128]{3,2,1,0:T(8,128)S(1)} %get-tuple-element.28), channel_id=1, source_target_pairs={{1,0},{2,1},{3,2},{4,3},{5,4},{6,5},{7,6},{9,8},{10,9},{11,10},{12... | collective-permute-start | bytes 589832 | tf_op jit(solution)/shard_map/ppermute | solution.py:21
  185.1 2.2 collective-permute-start.8
  187.3 0.0 collective-permute-done.11
  187.3 0.0 copy-start.5
  187.3 0.0 copy-start.7
  187.3 0.7 select_maximum_fusion.6
  188.1 0.2 collective-permute-done.9
  188.2 4.7 %collective-permute-done.8 = f32[3,2,64,128]{3,2,1,0:T(8,128)S(1)} collective-permute-done((f32[3,2,64,128]{3,2,1,0:T(8,128)S(1)}, f32[3,2,64,128]{3,2,1,0:T(8,128)S(1)}, u32[]{:S(2)}, u32[]{:S(2)}) %collective-permute-start.8) | collective-permute-done | bytes 196640 | tf_op jit(solution)/shard_map/ppermute | solution.py:19
  193.0 7.3 %select_maximum_fusion = f32[3,36,66,130]{3,2,1,0:T(8,128)S(1)} fusion(f32[3,2,64,128]{3,2,1,0:T(8,128)S(1)} %collective-permute-done.9, f32[3,2,64,128]{3,2,1,0:T(8,128)S(1)} %collective-permute-done.8, f32[1,32,64,128]{3,2,1,0:T(8,128)S(1)} %select_bitcast_fusion, f32[1,32,64,128]{3,2,1,0:T(8,128)S(1)} %get-tuple-element.17, f32[1,32,64,128]{3,2,1,0:T(8,128)S(1)} %bitcast.52), kind=kLoop, calls=%fused_computation.4 | loop fusion | flops 19459440 | bytes 7245504 | tf_op jit(solution)/shard_map/concatenate | solution.py:17
  200.2 0.7 slice_bitcast_fusion.2
  200.9 2.4 %multiply_add_fusion.1 = (f32[32,64,129]{2,1,0:T(8,128)S(1)}, f32[32,64,129]{2,1,0:T(8,128)S(1)}) fusion(f32[34,66,130]{2,1,0:T(8,128)S(1)} %select_maximum_fusion.6, f32[]{:T(128)} %bitcast.45, f32[34,66,130]{2,1,0:T(8,128)S(1)} %get-tuple-element.25, f32[34,66,130]{2,1,0:T(8,128)S(1)} %get-tuple-element.24, f32[]{:T(128)} %bitcast.42), kind=kLoop, calls=%fused_computation.30 | loop fusion | flops 3170304 | bytes 8454152 | tf_op jit(solution)/shard_map/add | solution.py:77
  203.3 0.0 copy-start.6
  203.3 0.0 copy-start.8
  203.3 1.9 multiply_add_fusion.3
  205.2 0.0 copy-start.4
  205.2 1.2 multiply_add_fusion.5
  206.5 2.1 fusion.21
  208.5 1.9 collective-permute-start.13
  210.4 2.6 %collective-permute-start.12 = (f32[1,64,128]{2,1,0:T(8,128)S(1)}, f32[1,64,128]{2,1,0:T(8,128)S(1)}, u32[]{:S(2)}, u32[]{:S(2)}) collective-permute-start(f32[1,64,128]{2,1,0:T(8,128)S(1)} %get-tuple-element.29), channel_id=1, source_target_pairs={{0,1},{1,2},{2,3},{3,4},{4,5},{5,6},{6,7},{8,9},{9,10},{10,11},{11... | collective-permute-start | bytes 98312 | tf_op jit(solution)/shard_map/ppermute | solution.py:19
  213.1 0.0 collective-permute-done.13
  213.1 3.5 %collective-permute-done.12 = f32[1,64,128]{2,1,0:T(8,128)S(1)} collective-permute-done((f32[1,64,128]{2,1,0:T(8,128)S(1)}, f32[1,64,128]{2,1,0:T(8,128)S(1)}, u32[]{:S(2)}, u32[]{:S(2)}) %collective-permute-start.12) | collective-permute-done | bytes 32800 | tf_op jit(solution)/shard_map/ppermute | solution.py:19
  216.6 0.7 select_maximum_fusion.4
  217.3 1.2 multiply_add_fusion
  218.5 0.7 multiply_add_fusion.2
  219.2 0.3 multiply_add_fusion.4
  219.5 1.9 fusion.13
  (20 shorter events, 0.1 us)
Async XLA Ops:
  7.2 23.3 %copy-start.1 = (f32[32,16,128]{2,1,0:T(8,128)S(1)}, f32[32,16,128]{2,1,0:T(8,128)}, u32[]{:S(2)}) copy-start(f32[32,16,128]{2,1,0:T(8,128)} %param.10) | copy-start | bytes 786436
  7.2 174.6 %all-gather.2.cloned.1.call-start = ((), (), s32[]{:S(2)}) async-start(), calls=%async_computation | async-start | bytes 1310720 | tf_op jit(solution)/shard_map/all_gather | solution.py:133
  15.0 5.9 %collective-permute-start.1 = (f32[32,1,128]{2,1,0:T(1,128)S(1)}, f32[32,1,128]{2,1,0:T(1,128)S(1)}, u32[]{:S(2)}, u32[]{:S(2)}) collective-permute-start(f32[32,1,128]{2,1,0:T(1,128)S(1)} %get-tuple-element.42), channel_id=1, source_target_pairs={{8,0},{16,8},{24,16},{9,1},{17,9},{25,17},{10,2},{18,10},{26,18},{... | collective-permute-start | bytes 49160 | tf_op jit(solution)/shard_map/ppermute | solution.py:21
  16.3 6.0 %collective-permute-start = (f32[32,1,128]{2,1,0:T(1,128)S(1)}, f32[32,1,128]{2,1,0:T(1,128)S(1)}, u32[]{:S(2)}, u32[]{:S(2)}) collective-permute-start(f32[32,1,128]{2,1,0:T(1,128)S(1)} %get-tuple-element.41), channel_id=1, source_target_pairs={{0,8},{8,16},{16,24},{1,9},{9,17},{17,25},{2,10},{10,18},{18,26},{... | collective-permute-start | bytes 49160 | tf_op jit(solution)/shard_map/ppermute | solution.py:19
  22.2 4.3 %collective-permute-start.2 = (f32[1,18,128]{2,1,0:T(8,128)S(1)}, f32[1,18,128]{2,1,0:T(8,128)S(1)}, u32[]{:S(2)}, u32[]{:S(2)}) collective-permute-start(f32[1,18,128]{2,1,0:T(8,128)S(1)} %get-tuple-element.38), channel_id=1, source_target_pairs={{1,0},{2,1},{3,2},{4,3},{5,4},{6,5},{7,6},{9,8},{10,9},{11,10},{12... | collective-permute-start | bytes 27656 | tf_op jit(solution)/shard_map/ppermute | solution.py:21
  24.2 5.9 %collective-permute-start.3 = (f32[1,18,128]{2,1,0:T(8,128)S(1)}, f32[1,18,128]{2,1,0:T(8,128)S(1)}, u32[]{:S(2)}, u32[]{:S(2)}) collective-permute-start(f32[1,18,128]{2,1,0:T(8,128)S(1)} %get-tuple-element.37), channel_id=1, source_target_pairs={{0,1},{1,2},{2,3},{3,4},{4,5},{5,6},{6,7},{8,9},{9,10},{10,11},{11... | collective-permute-start | bytes 27656 | tf_op jit(solution)/shard_map/ppermute | solution.py:19
  82.7 71.0 %copy-start = (f32[1,32,64,128]{3,2,1,0:T(8,128)S(1)}, f32[1,32,64,128]{3,2,1,0:T(8,128)}, u32[]{:S(2)}) copy-start(f32[1,32,64,128]{3,2,1,0:T(8,128)} %param.16) | copy-start | bytes 3145732
  82.7 6.1 %collective-permute-start.5 = (f32[32,1,128]{2,1,0:T(1,128)S(1)}, f32[32,1,128]{2,1,0:T(1,128)S(1)}, u32[]{:S(2)}, u32[]{:S(2)}) collective-permute-start(f32[32,1,128]{2,1,0:T(1,128)S(1)} %get-tuple-element.40), channel_id=1, source_target_pairs={{8,0},{16,8},{24,16},{9,1},{17,9},{25,17},{10,2},{18,10},{26,18},{... | collective-permute-start | bytes 49160 | tf_op jit(solution)/shard_map/ppermute | solution.py:21
  84.1 75.2 %copy-start.9 = (f32[1,3]{1,0:T(1,128)S(1)}, f32[1,3]{1,0:T(1,128)}, u32[]{:S(2)}) copy-start(f32[1,3]{1,0:T(1,128)} %param.13) | copy-start | bytes 40
  84.1 75.9 %copy-start.3 = (s32[32,64,128]{2,1,0:T(8,128)S(1)}, s32[32,64,128]{2,1,0:T(8,128)}, u32[]{:S(2)}) copy-start(s32[32,64,128]{2,1,0:T(8,128)} %param.9) | copy-start | bytes 3145732
  84.2 6.1 %collective-permute-start.4 = (f32[32,1,128]{2,1,0:T(1,128)S(1)}, f32[32,1,128]{2,1,0:T(1,128)S(1)}, u32[]{:S(2)}, u32[]{:S(2)}) collective-permute-start(f32[32,1,128]{2,1,0:T(1,128)S(1)} %get-tuple-element.39), channel_id=1, source_target_pairs={{0,8},{8,16},{16,24},{1,9},{9,17},{17,25},{2,10},{10,18},{18,26},{... | collective-permute-start | bytes 49160 | tf_op jit(solution)/shard_map/ppermute | solution.py:19
  90.3 4.3 %collective-permute-start.6 = (f32[1,18,128]{2,1,0:T(8,128)S(1)}, f32[1,18,128]{2,1,0:T(8,128)S(1)}, u32[]{:S(2)}, u32[]{:S(2)}) collective-permute-start(f32[1,18,128]{2,1,0:T(8,128)S(1)} %get-tuple-element.36), channel_id=1, source_target_pairs={{1,0},{2,1},{3,2},{4,3},{5,4},{6,5},{7,6},{9,8},{10,9},{11,10},{12... | collective-permute-start | bytes 27656 | tf_op jit(solution)/shard_map/ppermute | solution.py:21
  92.2 5.9 %collective-permute-start.7 = (f32[1,18,128]{2,1,0:T(8,128)S(1)}, f32[1,18,128]{2,1,0:T(8,128)S(1)}, u32[]{:S(2)}, u32[]{:S(2)}) collective-permute-start(f32[1,18,128]{2,1,0:T(8,128)S(1)} %get-tuple-element.35), channel_id=1, source_target_pairs={{0,1},{1,2},{2,3},{3,4},{4,5},{5,6},{6,7},{8,9},{9,10},{10,11},{11... | collective-permute-start | bytes 27656 | tf_op jit(solution)/shard_map/ppermute | solution.py:19
  153.7 33.6 %collective-permute-start.11 = (f32[1,64,128]{2,1,0:T(8,128)S(1)}, f32[1,64,128]{2,1,0:T(8,128)S(1)}, u32[]{:S(2)}, u32[]{:S(2)}) collective-permute-start(f32[1,64,128]{2,1,0:T(8,128)S(1)} %get-tuple-element.32), channel_id=1, source_target_pairs={{1,0},{2,1},{3,2},{4,3},{5,4},{6,5},{7,6},{9,8},{10,9},{11,10},{12... | collective-permute-start | bytes 98312 | tf_op jit(solution)/shard_map/ppermute | solution.py:21
  155.7 31.6 %collective-permute-start.10 = (f32[1,64,128]{2,1,0:T(8,128)S(1)}, f32[1,64,128]{2,1,0:T(8,128)S(1)}, u32[]{:S(2)}, u32[]{:S(2)}) collective-permute-start(f32[1,64,128]{2,1,0:T(8,128)S(1)} %get-tuple-element.31), channel_id=1, source_target_pairs={{0,1},{1,2},{2,3},{3,4},{4,5},{5,6},{6,7},{8,9},{9,10},{10,11},{11... | collective-permute-start | bytes 98312 | tf_op jit(solution)/shard_map/ppermute | solution.py:19
  182.6 10.3 %copy-start.2 = (f32[32,64,128]{2,1,0:T(8,128)S(1)}, f32[32,64,128]{2,1,0:T(8,128)}, u32[]{:S(2)}) copy-start(f32[32,64,128]{2,1,0:T(8,128)} %all-gather.2.cloned.1.call-done) | copy-start | bytes 3145732
  182.7 5.6 %collective-permute-start.9 = (f32[3,2,64,128]{3,2,1,0:T(8,128)S(1)}, f32[3,2,64,128]{3,2,1,0:T(8,128)S(1)}, u32[]{:S(2)}, u32[]{:S(2)}) collective-permute-start(f32[3,2,64,128]{3,2,1,0:T(8,128)S(1)} %get-tuple-element.28), channel_id=1, source_target_pairs={{1,0},{2,1},{3,2},{4,3},{5,4},{6,5},{7,6},{9,8},{10,9},{11,10},{12... | collective-permute-start | bytes 589832 | tf_op jit(solution)/shard_map/ppermute | solution.py:21
  185.1 7.9 %collective-permute-start.8 = (f32[3,2,64,128]{3,2,1,0:T(8,128)S(1)}, f32[3,2,64,128]{3,2,1,0:T(8,128)S(1)}, u32[]{:S(2)}, u32[]{:S(2)}) collective-permute-start(f32[3,2,64,128]{3,2,1,0:T(8,128)S(1)} %get-tuple-element.27), channel_id=1, source_target_pairs={{0,1},{1,2},{2,3},{3,4},{4,5},{5,6},{6,7},{8,9},{9,10},{10,11},{11... | collective-permute-start | bytes 589832 | tf_op jit(solution)/shard_map/ppermute | solution.py:19
  187.3 5.6 %copy-start.5 = (f32[1,64,128]{2,1,0:T(8,128)}, f32[1,64,128]{2,1,0:T(8,128)S(1)}, u32[]{:S(2)}) copy-start(f32[1,64,128]{2,1,0:T(8,128)S(1)} %collective-permute-done.11) | copy-start | bytes 98308
  187.3 5.6 %copy-start.7 = (f32[1,64,128]{2,1,0:T(8,128)}, f32[1,64,128]{2,1,0:T(8,128)S(1)}, u32[]{:S(2)}) copy-start(f32[1,64,128]{2,1,0:T(8,128)S(1)} %collective-permute-done.10) | copy-start | bytes 98308
  203.3 1.9 copy-start.6
  203.3 1.9 copy-start.8
  205.2 1.2 copy-start.4
  208.5 4.6 %collective-permute-start.13 = (f32[1,64,128]{2,1,0:T(8,128)S(1)}, f32[1,64,128]{2,1,0:T(8,128)S(1)}, u32[]{:S(2)}, u32[]{:S(2)}) collective-permute-start(f32[1,64,128]{2,1,0:T(8,128)S(1)} %get-tuple-element.30), channel_id=1, source_target_pairs={{1,0},{2,1},{3,2},{4,3},{5,4},{6,5},{7,6},{9,8},{10,9},{11,10},{12... | collective-permute-start | bytes 98312 | tf_op jit(solution)/shard_map/ppermute | solution.py:21
  210.4 6.1 %collective-permute-start.12 = (f32[1,64,128]{2,1,0:T(8,128)S(1)}, f32[1,64,128]{2,1,0:T(8,128)S(1)}, u32[]{:S(2)}, u32[]{:S(2)}) collective-permute-start(f32[1,64,128]{2,1,0:T(8,128)S(1)} %get-tuple-element.29), channel_id=1, source_target_pairs={{0,1},{1,2},{2,3},{3,4},{4,5},{5,6},{6,7},{8,9},{9,10},{10,11},{11... | collective-permute-start | bytes 98312 | tf_op jit(solution)/shard_map/ppermute | solution.py:19
Sparse Core Ops, SparseCore 0:
  153.8 27.8 all-gather.1
where the time goes:
time: 229 us; the launch traced here: 228 us
  blocking collectives  83 us (36%)
  other arithmetic  49.8 us (22%)
  waiting for transfers between devices  35.7 us (16%)
  starting transfers between devices  34.1 us (15%)
  between operations  21.4 us (9%)
  local copies, waits for them, and re-layouts  4.21 us (2%)
    psum x2, blocking collectives, paired_products(): lax.psum((jnp.sum(residual * precond), jnp.sum(precond * image)), ('size'...  83 us
    ppermute x7, starting transfers between devices, extended(): lax.ppermute(tail, axis, [(i, (i + 1) % count) for i in range(ends)])  21.2 us
    ppermute x7, waiting for transfers between devices, extended(): lax.ppermute(tail, axis, [(i, (i + 1) % count) for i in range(ends)])  18 us
    all_gather x1, waiting for transfers between devices, local(): slab_pressure = lax.all_gather(solution, 'size', axis=1, tiled=True)  17.5 us
    ppermute x7, starting transfers between devices, extended(): lax.ppermute(head, axis, [((i + 1) % count, i) for i in range(ends)])  12.8 us
    concatenate x7, other arithmetic, extended(): jnp.concatenate([lax.ppermute(tail, axis, [(i, (i + 1) % count) for i in...  9.57 us
    reduce_sum x2, other arithmetic, paired_products(): jnp.sum(precond * image)  9.51 us
    mul x2, other arithmetic, apply_operator(): scaled = conduct * vector  9.43 us
  transfers between devices with their start and end apart: 15, of which 8 were waited for; matrix products, arithmetic and copies ran while one was open for 3% of the time, Pallas kernels for 0%

commit v1 on v0

--- a/solution.py
+++ b/solution.py
@@ -130,7 +130,12 @@
             rho_now = rho_next
     conduct_slab = lookup(cond_table, tissue)
     rate_slab = lookup(bind_table[0], tissue)
-    slab_pressure = lax.all_gather(solution, "size", axis=1, tiled=True)
+    ring = [solution]
+    for hop in range(3):
+        ring.append(lax.ppermute(ring[-1], "size", [(dev, (dev + 1) % 4) for dev in range(4)]))
+    slab_pressure = jnp.roll(
+        jnp.concatenate(ring[::-1], axis=1), (lax.axis_index("size") + 1) * ring[0].shape[1], axis=1
+    )
     stacked = jnp.stack([slab_pressure, conduct_slab, rate_slab])
     rimmed = extended(stacked, (("gz", 1),), TSTEPS)
     fields_pad = jnp.pad(rimmed, ((0, 0), (0, 0), (1, 1), (1, 1)))

time: 229 us -> 215 us (0.939)
  between operations: 21.4 us -> 8.08 us
    all_gather x1 -> x0, waiting for transfers between devices: 17.5 us -> none  [local(): slab_pressure = lax.all_gather(solution, 'size', axis=1, tiled=True)]
    ppermute x0 -> x3, waiting for transfers between devices: none -> 15.8 us  [local(): lax.ppermute(ring[-1], 'size', [(dev, (dev + 1) % 4) for dev in range(4)])]
  transfers between devices with their start and end apart: 15 -> 17, of which waited for: 8 -> 10; matrix products, arithmetic and copies ran while one was open for 3% -> 3% of each run, Pallas kernels for 0% -> 0%
where the time goes in v1:
time: 215 us; the launch traced here: 214 us
  blocking collectives  83 us (39%)
  other arithmetic  49 us (23%)
  starting transfers between devices  35.3 us (16%)
  waiting for transfers between devices  34 us (16%)
  between operations  8.08 us (4%)
  local copies, waits for them, and re-layouts  4.47 us (2%)
    psum x2, blocking collectives, paired_products(): lax.psum((jnp.sum(residual * precond), jnp.sum(precond * image)), ('size'...  83 us
    ppermute x7, starting transfers between devices, extended(): lax.ppermute(tail, axis, [(i, (i + 1) % count) for i in range(ends)])  21.2 us
    ppermute x7, waiting for transfers between devices, extended(): lax.ppermute(tail, axis, [(i, (i + 1) % count) for i in range(ends)])  17.3 us
    ppermute x3, waiting for transfers between devices, local(): lax.ppermute(ring[-1], 'size', [(dev, (dev + 1) % 4) for dev in range(4)])  15.8 us
    ppermute x7, starting transfers between devices, extended(): lax.ppermute(head, axis, [((i + 1) % count, i) for i in range(ends)])  12.6 us
    reduce_sum x2, other arithmetic, paired_products(): jnp.sum(precond * image)  9.7 us
    mul x2, other arithmetic, apply_operator(): scaled = conduct * vector  9.7 us
    concatenate x7, other arithmetic, extended(): jnp.concatenate([lax.ppermute(tail, axis, [(i, (i + 1) % count) for i in...  9.55 us
  transfers between devices with their start and end apart: 17, of which 10 were waited for; matrix products, arithmetic and copies ran while one was open for 3% of the time, Pallas kernels for 0%

profile of v1, /device:TPU:4, one launch (start us, length us, event | category | flops | bytes accessed | tf_op | source)
XLA Modules:
  0.0 213.8 jit_solution(10435729309855684228)
XLA Ops:
  0.6 0.0 copy-start.1
  0.6 1.4 fusion.53
  2.1 1.4 fusion.52
  3.5 5.0 %fusion.39 = (f32[32,16,128]{2,1,0:T(8,128)S(1)}, pred[32,16,128]{2,1,0:T(8,128)(4,1)S(1)}, pred[32,16,128]{2,1,0:T(8,128)(4,1)S(1)}) fusion(f32[]{:T(128)} %bitcast.5, f32[]{:T(128)} %bitcast.4, f32[]{:T(128)} %bitcast.3, f32[32,16,128]{2,1,0:T(8,128)} %param.10, f32[]{:T(128)} %bitcast.2, f32[]{:T(128)} %bitcast.1, f32[]{:T(128)} %bitcast, ...), kind=kLoop, calls=%fused_computation.128 | loop fusion | flops 786432 | bytes 917532 | tf_op jit(solution)/shard_map/mul | solution.py:40
  8.6 1.3 collective-permute-start.1
  9.9 4.5 %collective-permute-start = (f32[32,1,128]{2,1,0:T(1,128)S(1)}, f32[32,1,128]{2,1,0:T(1,128)S(1)}, u32[]{:S(2)}, u32[]{:S(2)}) collective-permute-start(f32[32,1,128]{2,1,0:T(1,128)S(1)} %get-tuple-element.41), channel_id=1, source_target_pairs={{0,8},{8,16},{16,24},{1,9},{9,17},{17,25},{2,10},{10,18},{18,26},{... | collective-permute-start | bytes 49160 | tf_op jit(solution)/shard_map/ppermute | solution.py:19
  14.4 0.0 collective-permute-done.1
  14.4 1.4 collective-permute-done
  15.9 1.9 collective-permute-start.2
  17.8 2.4 %collective-permute-start.3 = (f32[1,18,128]{2,1,0:T(8,128)S(1)}, f32[1,18,128]{2,1,0:T(8,128)S(1)}, u32[]{:S(2)}, u32[]{:S(2)}) collective-permute-start(f32[1,18,128]{2,1,0:T(8,128)S(1)} %get-tuple-element.37), channel_id=1, source_target_pairs={{0,1},{1,2},{2,3},{3,4},{4,5},{5,6},{6,7},{8,9},{9,10},{10,11},{11... | collective-permute-start | bytes 27656 | tf_op jit(solution)/shard_map/ppermute | solution.py:19
  20.2 0.0 collective-permute-done.2
  20.2 3.5 %collective-permute-done.3 = f32[1,18,128]{2,1,0:T(8,128)S(1)} collective-permute-done((f32[1,18,128]{2,1,0:T(8,128)S(1)}, f32[1,18,128]{2,1,0:T(8,128)S(1)}, u32[]{:S(2)}, u32[]{:S(2)}) %collective-permute-start.3) | collective-permute-done | bytes 9248 | tf_op jit(solution)/shard_map/ppermute | solution.py:19
  23.7 0.4 select_maximum_fusion.12
  24.1 4.9 %multiply_reduce_fusion.1 = (f32[]{:T(128)}, f32[]{:T(128)}, f32[32,16,128]{2,1,0:T(8,128)S(1)}) fusion(pred[32,16,128]{2,1,0:T(8,128)(4,1)S(1)} %get-tuple-element.23, pred[32,16,128]{2,1,0:T(8,128)(4,1)S(1)} %get-tuple-element.22, f32[]{:T(128)} %bitcast.5, f32[]{:T(128)} %bitcast.4, f32[]{:T(128)} %bitcast.3, f32[32,16,128]{2,1,0:T(8,128)S(1)} %copy-done.1, ...), kind=kLoop, calls=%fused_computation.124 | loop fusion | flops 2031614 | bytes 1493024 | tf_op jit(solution)/shard_map/reduce_sum | solution.py:47
  29.0 41.5 %all-reduce.6 = (f32[]{:T(128)}, f32[]{:T(128)}) all-reduce(f32[]{:T(128)} %get-tuple-element.4, f32[]{:T(128)} %get-tuple-element.3), channel_id=1, replica_groups=mesh['size'=4,'gz'=8] {'size','gz'}, use_global_device_ids=true, to_apply=%region_1.2 | all-reduce | flops 2 | bytes 16 | tf_op jit(solution)/shard_map/psum | solution.py:47
  71.8 4.7 %fusion.38 = (f32[32,16,128]{2,1,0:T(8,128)S(1)}, f32[]{:T(128)}) fusion(pred[32,16,128]{2,1,0:T(8,128)(4,1)S(1)} %get-tuple-element.23, pred[32,16,128]{2,1,0:T(8,128)(4,1)S(1)} %get-tuple-element.22, f32[]{:T(128)} %bitcast.5, f32[]{:T(128)} %bitcast.4, f32[]{:T(128)} %bitcast.3, f32[32,16,128]{2,1,0:T(8,128)S(1)} %get-tuple-element.20, f32[]{:T(128)S(6)} %div.19, ...), kind=kLoop, calls=%fused_computation.127 | loop fusion | flops 917503 | bytes 917536 | tf_op jit(solution)/shard_map/mul | solution.py:40
  76.5 1.4 collective-permute-start.5
  77.9 4.5 %collective-permute-start.4 = (f32[32,1,128]{2,1,0:T(1,128)S(1)}, f32[32,1,128]{2,1,0:T(1,128)S(1)}, u32[]{:S(2)}, u32[]{:S(2)}) collective-permute-start(f32[32,1,128]{2,1,0:T(1,128)S(1)} %get-tuple-element.39), channel_id=1, source_target_pairs={{0,8},{8,16},{16,24},{1,9},{9,17},{17,25},{2,10},{10,18},{18,26},{... | collective-permute-start | bytes 49160 | tf_op jit(solution)/shard_map/ppermute | solution.py:19
  82.5 1.4 collective-permute-done.4
  83.9 1.9 collective-permute-start.6
  85.8 2.4 %collective-permute-start.7 = (f32[1,18,128]{2,1,0:T(8,128)S(1)}, f32[1,18,128]{2,1,0:T(8,128)S(1)}, u32[]{:S(2)}, u32[]{:S(2)}) collective-permute-start(f32[1,18,128]{2,1,0:T(8,128)S(1)} %get-tuple-element.35), channel_id=1, source_target_pairs={{0,1},{1,2},{2,3},{3,4},{4,5},{5,6},{6,7},{8,9},{9,10},{10,11},{11... | collective-permute-start | bytes 27656 | tf_op jit(solution)/shard_map/ppermute | solution.py:19
  88.2 3.5 %collective-permute-done.7 = f32[1,18,128]{2,1,0:T(8,128)S(1)} collective-permute-done((f32[1,18,128]{2,1,0:T(8,128)S(1)}, f32[1,18,128]{2,1,0:T(8,128)S(1)}, u32[]{:S(2)}, u32[]{:S(2)}) %collective-permute-start.7) | collective-permute-done | bytes 9248 | tf_op jit(solution)/shard_map/ppermute | solution.py:19
  91.7 0.4 select_maximum_fusion.8
  92.1 4.8 %fusion.28 = f32[]{:T(128)} fusion(f32[34,18,130]{2,1,0:T(8,128)S(1)} %select_maximum_fusion.8, f32[32,16,128]{2,1,0:T(8,128)S(1)} %get-tuple-element.33, f32[32,1,128]{2,1,0:T(1,128)S(1)} %collective-permute-done.4, f32[32,1,128]{2,1,0:T(1,128)S(1)} %collective-permute-done.5, f32[1,18,128]{2,1,0:T(8,128)S(1)} %collective-permute-done.7, ...), kind=kLoop, calls=%fused_computation.92 | loop fusion | flops 2031615 | bytes 1493024 | tf_op jit(solution)/shard_map/reduce_sum | solution.py:47
  97.0 41.4 %all-reduce.5 = (f32[]{:T(128)}, f32[]{:T(128)}) all-reduce(f32[]{:T(128)} %get-tuple-element.34, f32[]{:T(128)} %fusion.28), channel_id=1, replica_groups=mesh['size'=4,'gz'=8] {'size','gz'}, use_global_device_ids=true, to_apply=%region_5.6 | all-reduce | flops 2 | bytes 16 | tf_op jit(solution)/shard_map/psum | solution.py:47
  142.8 4.0 %multiply_add_fusion.6 = f32[32,16,128]{2,1,0:T(8,128)S(1)} fusion(f32[]{:T(128)S(6)} %div.21, f32[]{:T(128)S(6)} %div.23, f32[]{:T(128)S(6)} %div.19, pred[32,16,128]{2,1,0:T(8,128)(4,1)S(1)} %get-tuple-element.23, pred[32,16,128]{2,1,0:T(8,128)(4,1)S(1)} %get-tuple-element.22, f32[]{:T(128)} %bitcast.5, f32[]{:T(128)} %bitcast.4, f32[]{:T(128)} %bitcast.3, ...), kind=kLoop, calls=%fused_computation.121 | loop fusion | flops 1114112 | bytes 917540 | tf_op jit(solution)/shard_map/add | solution.py:120
  146.9 0.0 copy-start.2
  146.9 1.5 collective-permute-start.8
  148.3 7.6 %collective-permute-done.8 = f32[32,16,128]{2,1,0:T(8,128)S(1)} collective-permute-done((f32[32,16,128]{2,1,0:T(8,128)S(1)}, f32[32,16,128]{2,1,0:T(8,128)S(1)}, u32[]{:S(2)}, u32[]{:S(2)}) %collective-permute-start.8) | collective-permute-done | bytes 262176 | tf_op jit(solution)/shard_map/ppermute | solution.py:135
  156.0 0.0 collective-permute-start.9
  156.0 1.9 collective-permute-start.14
  157.9 2.4 %collective-permute-start.13 = (f32[1,64,128]{2,1,0:T(8,128)S(1)}, f32[1,64,128]{2,1,0:T(8,128)S(1)}, u32[]{:S(2)}, u32[]{:S(2)}) collective-permute-start(f32[1,64,128]{2,1,0:T(8,128)S(1)} %get-tuple-element.31), channel_id=1, source_target_pairs={{0,1},{1,2},{2,3},{3,4},{4,5},{5,6},{6,7},{8,9},{9,10},{10,11},{11... | collective-permute-start | bytes 98312 | tf_op jit(solution)/shard_map/ppermute | solution.py:19
  161.6 0.7 fusion.51
  162.3 1.8 collective-permute-done.9
  164.1 0.0 collective-permute-start.10
  164.1 2.3 %select_bitcast_fusion.1 = (f32[1,32,64,128]{3,2,1,0:T(8,128)S(1)}, pred[32,64,128]{2,1,0:T(8,128)(4,1)S(1)}, pred[32,64,128]{2,1,0:T(8,128)(4,1)S(1)}) fusion(f32[]{:T(128)} %bitcast.5, f32[]{:T(128)} %bitcast.4, f32[]{:T(128)} %bitcast.3, s32[32,64,128]{2,1,0:T(8,128)S(1)} %copy-done.3), kind=kLoop, calls=%fused_computation.70 | loop fusion | flops 1048576 | bytes 2621452 | tf_op jit(solution)/shard_map/stack | solution.py:139
  166.5 6.3 %collective-permute-done.10 = f32[32,16,128]{2,1,0:T(8,128)S(1)} collective-permute-done((f32[32,16,128]{2,1,0:T(8,128)S(1)}, f32[32,16,128]{2,1,0:T(8,128)S(1)}, u32[]{:S(2)}, u32[]{:S(2)}) %collective-permute-start.10) | collective-permute-done | bytes 262176 | tf_op jit(solution)/shard_map/ppermute | solution.py:135
  173.1 2.1 select_bitcast_fusion
  175.2 2.3 %collective-permute-start.12 = (f32[3,2,64,128]{3,2,1,0:T(8,128)S(1)}, f32[3,2,64,128]{3,2,1,0:T(8,128)S(1)}, u32[]{:S(2)}, u32[]{:S(2)}) collective-permute-start(f32[3,2,64,128]{3,2,1,0:T(8,128)S(1)} %get-tuple-element.28), channel_id=1, source_target_pairs={{1,0},{2,1},{3,2},{4,3},{5,4},{6,5},{7,6},{9,8},{10,9},{11,10},{12... | collective-permute-start | bytes 589832 | tf_op jit(solution)/shard_map/ppermute | solution.py:21
  177.5 2.2 %collective-permute-start.11 = (f32[3,2,64,128]{3,2,1,0:T(8,128)S(1)}, f32[3,2,64,128]{3,2,1,0:T(8,128)S(1)}, u32[]{:S(2)}, u32[]{:S(2)}) collective-permute-start(f32[3,2,64,128]{3,2,1,0:T(8,128)S(1)} %get-tuple-element.27), channel_id=1, source_target_pairs={{0,1},{1,2},{2,3},{3,4},{4,5},{5,6},{6,7},{8,9},{9,10},{10,11},{11... | collective-permute-start | bytes 589832 | tf_op jit(solution)/shard_map/ppermute | solution.py:19
  179.7 0.0 collective-permute-done.14
  179.7 0.0 copy-start.5
  179.8 0.0 copy-start.7
  179.8 0.7 select_maximum_fusion.6
  180.5 0.9 collective-permute-done.12
  181.4 4.0 %collective-permute-done.11 = f32[3,2,64,128]{3,2,1,0:T(8,128)S(1)} collective-permute-done((f32[3,2,64,128]{3,2,1,0:T(8,128)S(1)}, f32[3,2,64,128]{3,2,1,0:T(8,128)S(1)}, u32[]{:S(2)}, u32[]{:S(2)}) %collective-permute-start.11) | collective-permute-done | bytes 196640 | tf_op jit(solution)/shard_map/ppermute | solution.py:19
  185.4 7.2 %select_maximum_fusion = f32[3,36,66,130]{3,2,1,0:T(8,128)S(1)} fusion(f32[3,2,64,128]{3,2,1,0:T(8,128)S(1)} %collective-permute-done.12, f32[3,2,64,128]{3,2,1,0:T(8,128)S(1)} %collective-permute-done.11, f32[1,32,64,128]{3,2,1,0:T(8,128)S(1)} %get-tuple-element.52, f32[1,32,64,128]{3,2,1,0:T(8,128)S(1)} %get-tuple-element.17, ...), kind=kLoop, calls=%fused_computation.4 | loop fusion | flops 19459440 | bytes 7245504 | tf_op jit(solution)/shard_map/concatenate | solution.py:17
  192.6 0.7 slice_bitcast_fusion.2
  193.3 2.4 %multiply_add_fusion.1 = (f32[32,64,129]{2,1,0:T(8,128)S(1)}, f32[32,64,129]{2,1,0:T(8,128)S(1)}) fusion(f32[34,66,130]{2,1,0:T(8,128)S(1)} %select_maximum_fusion.6, f32[]{:T(128)} %bitcast.46, f32[34,66,130]{2,1,0:T(8,128)S(1)} %get-tuple-element.25, f32[34,66,130]{2,1,0:T(8,128)S(1)} %get-tuple-element.24, f32[]{:T(128)} %bitcast.43), kind=kLoop, calls=%fused_computation.30 | loop fusion | flops 3170304 | bytes 8454152 | tf_op jit(solution)/shard_map/add | solution.py:77
  195.7 0.0 copy-start.6
  195.7 0.0 copy-start.8
  195.7 1.9 multiply_add_fusion.3
  197.6 0.0 copy-start.4
  197.6 1.2 multiply_add_fusion.5
  198.9 2.1 fusion.21
  200.9 1.9 collective-permute-start.16
  202.8 2.6 %collective-permute-start.15 = (f32[1,64,128]{2,1,0:T(8,128)S(1)}, f32[1,64,128]{2,1,0:T(8,128)S(1)}, u32[]{:S(2)}, u32[]{:S(2)}) collective-permute-start(f32[1,64,128]{2,1,0:T(8,128)S(1)} %get-tuple-element.29), channel_id=1, source_target_pairs={{0,1},{1,2},{2,3},{3,4},{4,5},{5,6},{6,7},{8,9},{9,10},{10,11},{11... | collective-permute-start | bytes 98312 | tf_op jit(solution)/shard_map/ppermute | solution.py:19
  205.5 0.0 collective-permute-done.16
  205.5 3.5 %collective-permute-done.15 = f32[1,64,128]{2,1,0:T(8,128)S(1)} collective-permute-done((f32[1,64,128]{2,1,0:T(8,128)S(1)}, f32[1,64,128]{2,1,0:T(8,128)S(1)}, u32[]{:S(2)}, u32[]{:S(2)}) %collective-permute-start.15) | collective-permute-done | bytes 32800 | tf_op jit(solution)/shard_map/ppermute | solution.py:19
  209.0 0.7 select_maximum_fusion.4
  209.7 1.2 multiply_add_fusion
  210.9 0.7 multiply_add_fusion.2
  211.6 0.3 multiply_add_fusion.4
  211.9 1.9 fusion.13
  (31 shorter events, 0.3 us)
Async XLA Ops:
  0.6 23.5 %copy-start.1 = (f32[32,16,128]{2,1,0:T(8,128)S(1)}, f32[32,16,128]{2,1,0:T(8,128)}, u32[]{:S(2)}) copy-start(f32[32,16,128]{2,1,0:T(8,128)} %param.10) | copy-start | bytes 786436
  8.6 5.9 %collective-permute-start.1 = (f32[32,1,128]{2,1,0:T(1,128)S(1)}, f32[32,1,128]{2,1,0:T(1,128)S(1)}, u32[]{:S(2)}, u32[]{:S(2)}) collective-permute-start(f32[32,1,128]{2,1,0:T(1,128)S(1)} %get-tuple-element.42), channel_id=1, source_target_pairs={{8,0},{16,8},{24,16},{9,1},{17,9},{25,17},{10,2},{18,10},{26,18},{... | collective-permute-start | bytes 49160 | tf_op jit(solution)/shard_map/ppermute | solution.py:21
  9.9 6.0 %collective-permute-start = (f32[32,1,128]{2,1,0:T(1,128)S(1)}, f32[32,1,128]{2,1,0:T(1,128)S(1)}, u32[]{:S(2)}, u32[]{:S(2)}) collective-permute-start(f32[32,1,128]{2,1,0:T(1,128)S(1)} %get-tuple-element.41), channel_id=1, source_target_pairs={{0,8},{8,16},{16,24},{1,9},{9,17},{17,25},{2,10},{10,18},{18,26},{... | collective-permute-start | bytes 49160 | tf_op jit(solution)/shard_map/ppermute | solution.py:19
  15.9 4.3 %collective-permute-start.2 = (f32[1,18,128]{2,1,0:T(8,128)S(1)}, f32[1,18,128]{2,1,0:T(8,128)S(1)}, u32[]{:S(2)}, u32[]{:S(2)}) collective-permute-start(f32[1,18,128]{2,1,0:T(8,128)S(1)} %get-tuple-element.38), channel_id=1, source_target_pairs={{1,0},{2,1},{3,2},{4,3},{5,4},{6,5},{7,6},{9,8},{10,9},{11,10},{12... | collective-permute-start | bytes 27656 | tf_op jit(solution)/shard_map/ppermute | solution.py:21
  17.8 5.9 %collective-permute-start.3 = (f32[1,18,128]{2,1,0:T(8,128)S(1)}, f32[1,18,128]{2,1,0:T(8,128)S(1)}, u32[]{:S(2)}, u32[]{:S(2)}) collective-permute-start(f32[1,18,128]{2,1,0:T(8,128)S(1)} %get-tuple-element.37), channel_id=1, source_target_pairs={{0,1},{1,2},{2,3},{3,4},{4,5},{5,6},{6,7},{8,9},{9,10},{10,11},{11... | collective-permute-start | bytes 27656 | tf_op jit(solution)/shard_map/ppermute | solution.py:19
  76.4 79.5 %copy-start = (f32[1,32,64,128]{3,2,1,0:T(8,128)S(1)}, f32[1,32,64,128]{3,2,1,0:T(8,128)}, u32[]{:S(2)}) copy-start(f32[1,32,64,128]{3,2,1,0:T(8,128)} %param.16) | copy-start | bytes 3145732
  76.4 85.2 %copy-start.9 = (f32[1,3]{1,0:T(1,128)S(1)}, f32[1,3]{1,0:T(1,128)}, u32[]{:S(2)}) copy-start(f32[1,3]{1,0:T(1,128)} %param.13) | copy-start | bytes 40
  76.4 87.7 %copy-start.3 = (s32[32,64,128]{2,1,0:T(8,128)S(1)}, s32[32,64,128]{2,1,0:T(8,128)}, u32[]{:S(2)}) copy-start(s32[32,64,128]{2,1,0:T(8,128)} %param.9) | copy-start | bytes 3145732
  76.5 6.0 %collective-permute-start.5 = (f32[32,1,128]{2,1,0:T(1,128)S(1)}, f32[32,1,128]{2,1,0:T(1,128)S(1)}, u32[]{:S(2)}, u32[]{:S(2)}) collective-permute-start(f32[32,1,128]{2,1,0:T(1,128)S(1)} %get-tuple-element.40), channel_id=1, source_target_pairs={{8,0},{16,8},{24,16},{9,1},{17,9},{25,17},{10,2},{18,10},{26,18},{... | collective-permute-start | bytes 49160 | tf_op jit(solution)/shard_map/ppermute | solution.py:21
  77.9 6.0 %collective-permute-start.4 = (f32[32,1,128]{2,1,0:T(1,128)S(1)}, f32[32,1,128]{2,1,0:T(1,128)S(1)}, u32[]{:S(2)}, u32[]{:S(2)}) collective-permute-start(f32[32,1,128]{2,1,0:T(1,128)S(1)} %get-tuple-element.39), channel_id=1, source_target_pairs={{0,8},{8,16},{16,24},{1,9},{9,17},{17,25},{2,10},{10,18},{18,26},{... | collective-permute-start | bytes 49160 | tf_op jit(solution)/shard_map/ppermute | solution.py:19
  83.9 4.3 %collective-permute-start.6 = (f32[1,18,128]{2,1,0:T(8,128)S(1)}, f32[1,18,128]{2,1,0:T(8,128)S(1)}, u32[]{:S(2)}, u32[]{:S(2)}) collective-permute-start(f32[1,18,128]{2,1,0:T(8,128)S(1)} %get-tuple-element.36), channel_id=1, source_target_pairs={{1,0},{2,1},{3,2},{4,3},{5,4},{6,5},{7,6},{9,8},{10,9},{11,10},{12... | collective-permute-start | bytes 27656 | tf_op jit(solution)/shard_map/ppermute | solution.py:21
  85.8 5.9 %collective-permute-start.7 = (f32[1,18,128]{2,1,0:T(8,128)S(1)}, f32[1,18,128]{2,1,0:T(8,128)S(1)}, u32[]{:S(2)}, u32[]{:S(2)}) collective-permute-start(f32[1,18,128]{2,1,0:T(8,128)S(1)} %get-tuple-element.35), channel_id=1, source_target_pairs={{0,1},{1,2},{2,3},{3,4},{4,5},{5,6},{6,7},{8,9},{9,10},{10,11},{11... | collective-permute-start | bytes 27656 | tf_op jit(solution)/shard_map/ppermute | solution.py:19
  146.9 26.2 %copy-start.2 = (f32[32,16,128]{2,1,0:T(8,128)}, f32[32,16,128]{2,1,0:T(8,128)S(1)}, u32[]{:S(2)}) copy-start(f32[32,16,128]{2,1,0:T(8,128)S(1)} %multiply_add_fusion.6) | copy-start | bytes 786436
  146.9 9.1 %collective-permute-start.8 = (f32[32,16,128]{2,1,0:T(8,128)S(1)}, f32[32,16,128]{2,1,0:T(8,128)S(1)}, u32[]{:S(2)}, u32[]{:S(2)}) collective-permute-start(f32[32,16,128]{2,1,0:T(8,128)S(1)} %multiply_add_fusion.6), channel_id=1, source_target_pairs={{0,8},{8,16},{16,24},{24,0},{1,9},{9,17},{17,25},{25,1},{2,10},{10... | collective-permute-start | bytes 786440 | tf_op jit(solution)/shard_map/ppermute | solution.py:135
  156.0 8.2 %collective-permute-start.9 = (f32[32,16,128]{2,1,0:T(8,128)S(1)}, f32[32,16,128]{2,1,0:T(8,128)S(1)}, u32[]{:S(2)}, u32[]{:S(2)}) collective-permute-start(f32[32,16,128]{2,1,0:T(8,128)S(1)} %collective-permute-done.8), channel_id=1, source_target_pairs={{0,8},{8,16},{16,24},{24,0},{1,9},{9,17},{17,25},{25,1},{2,10},{10... | collective-permute-start | bytes 786440 | tf_op jit(solution)/shard_map/ppermute | solution.py:135
  156.0 23.7 %collective-permute-start.14 = (f32[1,64,128]{2,1,0:T(8,128)S(1)}, f32[1,64,128]{2,1,0:T(8,128)S(1)}, u32[]{:S(2)}, u32[]{:S(2)}) collective-permute-start(f32[1,64,128]{2,1,0:T(8,128)S(1)} %get-tuple-element.32), channel_id=1, source_target_pairs={{1,0},{2,1},{3,2},{4,3},{5,4},{6,5},{7,6},{9,8},{10,9},{11,10},{12... | collective-permute-start | bytes 98312 | tf_op jit(solution)/shard_map/ppermute | solution.py:21
  157.9 21.8 %collective-permute-start.13 = (f32[1,64,128]{2,1,0:T(8,128)S(1)}, f32[1,64,128]{2,1,0:T(8,128)S(1)}, u32[]{:S(2)}, u32[]{:S(2)}) collective-permute-start(f32[1,64,128]{2,1,0:T(8,128)S(1)} %get-tuple-element.31), channel_id=1, source_target_pairs={{0,1},{1,2},{2,3},{3,4},{4,5},{5,6},{6,7},{8,9},{9,10},{10,11},{11... | collective-permute-start | bytes 98312 | tf_op jit(solution)/shard_map/ppermute | solution.py:19
  164.1 8.7 %collective-permute-start.10 = (f32[32,16,128]{2,1,0:T(8,128)S(1)}, f32[32,16,128]{2,1,0:T(8,128)S(1)}, u32[]{:S(2)}, u32[]{:S(2)}) collective-permute-start(f32[32,16,128]{2,1,0:T(8,128)S(1)} %collective-permute-done.9), channel_id=1, source_target_pairs={{0,8},{8,16},{16,24},{24,0},{1,9},{9,17},{17,25},{25,1},{2,10},{10... | collective-permute-start | bytes 786440 | tf_op jit(solution)/shard_map/ppermute | solution.py:135
  175.2 6.2 %collective-permute-start.12 = (f32[3,2,64,128]{3,2,1,0:T(8,128)S(1)}, f32[3,2,64,128]{3,2,1,0:T(8,128)S(1)}, u32[]{:S(2)}, u32[]{:S(2)}) collective-permute-start(f32[3,2,64,128]{3,2,1,0:T(8,128)S(1)} %get-tuple-element.28), channel_id=1, source_target_pairs={{1,0},{2,1},{3,2},{4,3},{5,4},{6,5},{7,6},{9,8},{10,9},{11,10},{12... | collective-permute-start | bytes 589832 | tf_op jit(solution)/shard_map/ppermute | solution.py:21
  177.5 7.9 %collective-permute-start.11 = (f32[3,2,64,128]{3,2,1,0:T(8,128)S(1)}, f32[3,2,64,128]{3,2,1,0:T(8,128)S(1)}, u32[]{:S(2)}, u32[]{:S(2)}) collective-permute-start(f32[3,2,64,128]{3,2,1,0:T(8,128)S(1)} %get-tuple-element.27), channel_id=1, source_target_pairs={{0,1},{1,2},{2,3},{3,4},{4,5},{5,6},{6,7},{8,9},{9,10},{10,11},{11... | collective-permute-start | bytes 589832 | tf_op jit(solution)/shard_map/ppermute | solution.py:19
  179.7 5.6 %copy-start.5 = (f32[1,64,128]{2,1,0:T(8,128)}, f32[1,64,128]{2,1,0:T(8,128)S(1)}, u32[]{:S(2)}) copy-start(f32[1,64,128]{2,1,0:T(8,128)S(1)} %collective-permute-done.14) | copy-start | bytes 98308
  179.8 5.6 %copy-start.7 = (f32[1,64,128]{2,1,0:T(8,128)}, f32[1,64,128]{2,1,0:T(8,128)S(1)}, u32[]{:S(2)}) copy-start(f32[1,64,128]{2,1,0:T(8,128)S(1)} %collective-permute-done.13) | copy-start | bytes 98308
  195.7 1.9 copy-start.6
  195.7 1.9 copy-start.8
  197.6 1.2 copy-start.4
  200.9 4.6 %collective-permute-start.16 = (f32[1,64,128]{2,1,0:T(8,128)S(1)}, f32[1,64,128]{2,1,0:T(8,128)S(1)}, u32[]{:S(2)}, u32[]{:S(2)}) collective-permute-start(f32[1,64,128]{2,1,0:T(8,128)S(1)} %get-tuple-element.30), channel_id=1, source_target_pairs={{1,0},{2,1},{3,2},{4,3},{5,4},{6,5},{7,6},{9,8},{10,9},{11,10},{12... | collective-permute-start | bytes 98312 | tf_op jit(solution)/shard_map/ppermute | solution.py:21
  202.8 6.1 %collective-permute-start.15 = (f32[1,64,128]{2,1,0:T(8,128)S(1)}, f32[1,64,128]{2,1,0:T(8,128)S(1)}, u32[]{:S(2)}, u32[]{:S(2)}) collective-permute-start(f32[1,64,128]{2,1,0:T(8,128)S(1)} %get-tuple-element.29), channel_id=1, source_target_pairs={{0,1},{1,2},{2,3},{3,4},{4,5},{5,6},{6,7},{8,9},{9,10},{10,11},{11... | collective-permute-start | bytes 98312 | tf_op jit(solution)/shard_map/ppermute | solution.py:19
